TPU v7x, 32 devices: a whole 2x2x4 slice. The times are simulated.
32 devices in a mesh: rep: 4 (over z), px: 4 (over x, core), py: 2 (over y).
Axes of the slice: x: 2, y: 2, z: 4, core: 2. Of those that a mesh axis runs over, the one named last changes fastest.
Arguments:
- state: float32 [12, 2, 192, 96, 256], P('rep', None, 'px', 'py'), parts along dimension 0, may hold values from -6 to 6
- cotangent: float32 [12, 2, 192, 96, 256], P('rep', None, 'px', 'py'), parts along dimension 0, may hold values from -6 to 6
- w_in: bfloat16 [512, 192], replicated, may hold values from -0.4375 to 0.4375
- b_in: float32 [512], replicated, may hold values from -5 to 5
- w_out: bfloat16 [192, 512], replicated, may hold values from -0.25 to 0.25
Outputs:
- state_grad: float32 [12, 2, 192, 96, 256], P('rep', None, 'px', 'py'), parts along dimension 0
- grad_in: float32 [512, 768], P(('px', 'py'), 'rep'), parts along dimension 1
- grad_out: float32 [768, 512], P('rep', ('px', 'py')), parts along dimension 0
- grad_bias: float32 [4, 512], P('rep', ('px', 'py')), parts along dimension 0
There are 4 independent parts, one for each index of `rep`. A program takes and returns all parts, laid end to end along the dimension named above; an argument that names none is the same for every part. Nothing has to cross between parts.
All inputs are finite; a program needn't handle non-finite values.
Results may differ from a plain program's by a relative error of at most 0.0065.
The roundings to bfloat16 on the way count: a program that leaves them out, or rounds other values in their place, can miss the bound.
Values may be sent and summed in bfloat16 or wider, within the bound.
A program may use at most 448 MiB of HBM per device.

v0:
```python
import math

import jax
import jax.numpy as jnp
from jax import lax
from jax.sharding import PartitionSpec as P

PATCH = 4


NU_DT = 5e-05
TIME_STEP = 0.01
FORCING = 20.0


def angles(leading, trailing, length):
    product = leading[:, None] * trailing[None, :] % length
    phases = product.astype(jnp.float32) * (2.0 * math.pi / length)
    factor = 1.0 / math.sqrt(length)
    return (jnp.cos(phases) * factor, jnp.sin(phases) * factor)


def mode_ids(count, length):
    counter = jnp.arange(count, dtype=jnp.int32)
    return jnp.where(counter < count // 2, counter, counter + length - count)


def mode_table(modes, length, direction):
    cosine, sine_part = angles(modes, jnp.arange(length, dtype=jnp.int32), length)
    top_rows = jnp.stack([cosine, direction * sine_part], axis=1)
    low_rows = jnp.stack([-direction * sine_part, cosine], axis=1)
    return jnp.stack([top_rows, low_rows], axis=0).astype(jnp.bfloat16)


def complex_table(length, direction):
    return mode_table(jnp.arange(length, dtype=jnp.int32), length, direction)


def real_table(length, mode_count):
    cosine, sine_part = angles(
        jnp.arange(mode_count, dtype=jnp.int32), jnp.arange(length, dtype=jnp.int32), length
    )
    return jnp.stack([cosine, -sine_part], axis=0).astype(jnp.bfloat16)


def box_order(length, span):
    counter = jnp.arange(length, dtype=jnp.int32)
    local = counter % span
    rows = span // PATCH
    return counter - local + local % rows * PATCH + local // rows


def signed(counter, length):
    return jnp.where(counter < length // 2, counter, counter - length).astype(jnp.float32)


def factors(ky_ids, kz_ids, length, ky_count):
    cutoff = length // 3
    wave_y = signed(ky_ids, ky_count)[:, None, None]
    wave_z = kz_ids.astype(jnp.float32)[None, :, None]
    wave_x = signed(jnp.arange(length, dtype=jnp.int32), length)[None, None, :]
    retained = (
        (jnp.abs(wave_x) <= cutoff) & (jnp.abs(wave_y) <= cutoff) & (wave_z <= cutoff)
    ).astype(jnp.float32)
    square = wave_x * wave_x + wave_y * wave_y + wave_z * wave_z
    damping = jnp.exp(-NU_DT * square)
    weight = jnp.where(kz_ids[None, :, None] == 0, 1.0, 2.0).astype(jnp.float32)
    return ((wave_x, wave_y, wave_z), retained, damping, weight, square)


def cross(former, latter):
    return [
        former[1] * latter[2] - former[2] * latter[1],
        former[2] * latter[0] - former[0] * latter[2],
        former[0] * latter[1] - former[1] * latter[0],
    ]


def curl_modes(waves, spectra):
    real_part = cross(waves, [spectra[slot, 0] for slot in range(3)])
    imag_part = cross(waves, [spectra[slot, 1] for slot in range(3)])
    return jnp.stack([jnp.stack([-imag_part[slot], real_part[slot]]) for slot in range(3)])


def project(waves, square, spectra):
    dotted = waves[0] * spectra[0] + waves[1] * spectra[1] + waves[2] * spectra[2]
    along_k = dotted / jnp.maximum(square, 1.0)
    return jnp.stack([spectra[slot] - waves[slot] * along_k for slot in range(3)])


def to_physical(spectra):
    channels, paired, width_y, width_z, length = spectra.shape
    parts_x = lax.axis_size("px")
    parts_y = lax.axis_size("py")
    order_y = box_order(length, length)
    order_z = box_order(length, length)
    inverse = complex_table(length, 1.0)
    y_table = mode_table(mode_ids(width_y * parts_x, length), length, 1.0)[..., order_y].reshape(
        2, parts_x, width_y, 2, length
    )
    z_table = real_table(length, width_z * parts_y)[..., order_z].reshape(
        2, parts_y, width_z, length
    )
    flat = spectra.astype(jnp.bfloat16).reshape(channels, paired, width_y * width_z, length)
    along_x = jnp.einsum(
        "crpn,rnsx->csxp", flat, inverse, preferred_element_type=jnp.float32
    ).astype(jnp.bfloat16)
    along_x = along_x.reshape(channels, 2, length, 1, width_y * width_z)
    moved = lax.all_to_all(along_x, ("px", "py"), split_axis=2, concat_axis=3, tiled=True)
    blocks = moved.reshape(moved.shape[0], 2, moved.shape[2], parts_x, parts_y, width_y, width_z)
    along_y = jnp.einsum(
        "csxjlam,sjaty->cxtlmy", blocks, y_table, preferred_element_type=jnp.float32
    ).astype(jnp.bfloat16)
    return jnp.einsum(
        "cxtlmy,tlmz->cxyz", along_y, z_table, preferred_element_type=jnp.float32
    ).astype(jnp.bfloat16)


def to_spectral(field, ky_count, mode_count):
    channels, span_x, span_y, length = field.shape
    parts_x = lax.axis_size("px")
    parts_y = lax.axis_size("py")
    width_y = ky_count // parts_x
    width_z = mode_count // parts_y
    order_y = box_order(length, span_y)
    order_z = box_order(length, length)
    forward = complex_table(length, -1.0)
    y_table = (
        mode_table(mode_ids(ky_count, length), length, -1.0)
        .transpose(0, 3, 2, 1)[:, order_y]
        .reshape(2, length, 2, parts_x, width_y)
    )
    z_table = real_table(length, mode_count)[..., order_z].reshape(2, parts_y, width_z, length)
    along_z = jnp.einsum(
        "cxyz,rlmz->crlmxy", field, z_table, preferred_element_type=jnp.float32
    ).astype(jnp.bfloat16)
    along_y = jnp.einsum(
        "crlmxy,rysja->csxjlam", along_z, y_table, preferred_element_type=jnp.float32
    ).astype(jnp.bfloat16)
    along_y = along_y.reshape(channels, 2, span_x, parts_x * parts_y, width_y * width_z)
    moved = lax.all_to_all(along_y, ("px", "py"), split_axis=3, concat_axis=2, tiled=True)
    number = moved.shape[0]
    flat = moved.reshape(number, 2, length, -1)
    along_x = jnp.einsum("csxp,sxtn->ctpn", flat, forward, preferred_element_type=jnp.float32)
    return along_x.reshape(number, 2, width_y, width_z, length)


def to_boxes(field):
    channels, span_x, span_y, span_z = field.shape
    tiles = field.reshape(
        channels, span_x // PATCH, PATCH, PATCH, span_y // PATCH, PATCH, span_z // PATCH
    )
    return tiles.transpose(0, 2, 3, 5, 1, 4, 6).reshape(channels * PATCH**3, -1)


def from_boxes(box_values, layout):
    channels, span_x, span_y, span_z = layout
    tiles = box_values.reshape(
        channels, PATCH, PATCH, PATCH, span_x // PATCH, span_y // PATCH, span_z // PATCH
    )
    return tiles.transpose(0, 4, 1, 2, 5, 3, 6).reshape(layout)


def closure_terms(velocity, force_adj, w_in, b_in, w_out):
    features = to_boxes(velocity)
    adjoints = to_boxes(force_adj)
    pre_act = jnp.dot(w_in, features, preferred_element_type=jnp.float32) + b_in[:, None]
    hidden = jax.nn.silu(pre_act).astype(jnp.bfloat16)
    sigmoid = jax.nn.sigmoid(pre_act)
    hidden_adj = FORCING * jnp.dot(w_out.T, adjoints, preferred_element_type=jnp.float32)
    pre_adj = (hidden_adj * sigmoid * (1.0 + pre_act * (1.0 - sigmoid))).astype(jnp.bfloat16)
    grad_in = jnp.dot(pre_adj, features.T, preferred_element_type=jnp.float32)
    grad_out = FORCING * jnp.dot(adjoints, hidden.T, preferred_element_type=jnp.float32)
    grad_bias = jnp.sum(pre_adj.astype(jnp.float32), axis=1)[None, :]
    feat_adj = jnp.dot(w_in.T, pre_adj, preferred_element_type=jnp.float32)
    return (from_boxes(feat_adj, velocity.shape), grad_in, grad_out, grad_bias)


def pointwise(feat_adj, velocity, vorticity, force_adj):
    vel_list = [velocity[slot].astype(jnp.float32) for slot in range(3)]
    vort_list = [vorticity[slot].astype(jnp.float32) for slot in range(3)]
    force_list = [force_adj[slot].astype(jnp.float32) for slot in range(3)]
    turned = cross(vort_list, force_list)
    vel_adj = jnp.stack([feat_adj[slot] + turned[slot] for slot in range(3)]).astype(jnp.bfloat16)
    vort_adj = jnp.stack(cross(force_list, vel_list)).astype(jnp.bfloat16)
    return (vel_adj, vort_adj)


def shards(state, cotangent, w_in, b_in, w_out):
    width_y = state.shape[2]
    width_z = state.shape[3]
    length = state.shape[4]
    ky_count = width_y * lax.axis_size("px")
    ky_ids = lax.axis_index("px") * width_y + jnp.arange(width_y, dtype=jnp.int32)
    kz_ids = lax.axis_index("py") * width_z + jnp.arange(width_z, dtype=jnp.int32)
    waves, retained, damping, weight, square = factors(ky_ids, kz_ids, length, ky_count)
    kept = retained * state
    spectra = weight * jnp.concatenate([kept, curl_modes(waves, kept)], axis=0)
    force_spec = TIME_STEP * retained * project(waves, square, damping * cotangent)
    fields = to_physical(spectra)
    velocity, vorticity = (fields[:3], fields[3:])
    force_adj = to_physical(force_spec)
    feat_adj, grad_in, grad_out, grad_bias = closure_terms(velocity, force_adj, w_in, b_in, w_out)
    vel_adj, vort_adj = pointwise(feat_adj, velocity, vorticity, force_adj)
    spectral = to_spectral(
        jnp.concatenate([vel_adj, vort_adj], axis=0), ky_count, width_z * lax.axis_size("py")
    )
    state_grad = damping * cotangent + weight * retained * (
        spectral[:3] + curl_modes(waves, spectral[3:])
    )
    grad_in, grad_out, grad_bias = (
        lax.psum_scatter(grad_in, ("px", "py"), scatter_dimension=0, tiled=True),
        lax.psum_scatter(grad_out, ("px", "py"), scatter_dimension=1, tiled=True),
        lax.psum_scatter(grad_bias, ("px", "py"), scatter_dimension=1, tiled=True),
    )
    return (state_grad, grad_in, grad_out, grad_bias)


def solution(mesh):
    return jax.shard_map(
        shards,
        mesh=mesh,
        in_specs=(
            P("rep", None, "px", "py", None),
            P("rep", None, "px", "py", None),
            P(),
            P(),
            P(),
        ),
        out_specs=(
            P("rep", None, "px", "py", None),
            P(("px", "py"), "rep"),
            P("rep", ("px", "py")),
            P("rep", ("px", "py")),
        ),
        check_vma=False,
    )
```

profile of v0, /device:TPU:0, one launch (start us, length us, event | category | flops | bytes accessed | tf_op | source)
XLA Modules:
  0.0 1269.2 jit_solution(7051030765421699349)
XLA Ops:
  46.3 23.6 %copy.130 = bf16[3,2,256,1,2304]{4,1,3,0,2:T(2,128)(2,1)} copy(bf16[3,2,256,1,2304]{4,2,0,1,3:T(8,128)(2,1)S(1)} %fusion.58) | data formatting | bytes 14155776 | tf_op jit(solution)/shard_map/reshape | solution.py:108
  123.5 26.6 %copy.136 = bf16[6,2,256,1,2304]{4,1,3,0,2:T(2,128)(2,1)} copy(bf16[6,2,256,1,2304]{4,2,0,1,3:T(8,128)(2,1)} %fusion.25) | data formatting | bytes 28311552 | tf_op jit(solution)/shard_map/reshape | solution.py:108
  181.4 28.9 %reshape.1115 = bf16[3,2,32,4,2,48,48]{6,5,4,3,2,1,0:T(8,128)(2,1)} reshape(bf16[3,2,32,8,1,2304]{5,3,2,1,0,4:T(8,128)(2,1)} %bitcast.337) | data formatting | bytes 14155776 | tf_op jit(solution)/shard_map/reshape | solution.py:110
  226.6 36.2 %reshape.1116 = bf16[3,8,4,4,64,4,64]{6,5,4,3,2,1,0:T(4,128)(2,1)} reshape(bf16[3,32,256,256]{3,2,1,0:T(8,128)(2,1)} %bitcast_convert_fusion.4) | data formatting | bytes 25165824 | tf_op jit(solution)/shard_map/reshape | solution.py:150
  262.8 22.6 %copy.228 = bf16[3,8,4,4,64,4,64]{6,4,1,5,3,2,0:T(8,128)(2,1)} copy(bf16[3,8,4,4,64,4,64]{6,5,4,3,2,1,0:T(4,128)(2,1)} %reshape.1116) | data formatting | bytes 25165824 | tf_op jit(solution)/shard_map/reshape | solution.py:150
  285.4 29.1 %reshape.1117 = bf16[192,32768]{1,0:T(8,128)(2,1)} reshape(bf16[3,4,4,4,8,64,64]{6,5,4,3,2,1,0:T(8,128)(2,1)} %bitcast.326) | data formatting | bytes 25165824 | tf_op jit(solution)/shard_map/reshape | solution.py:153
  327.4 56.1 %reshape.1119 = bf16[6,2,32,4,2,48,48]{6,5,4,3,2,1,0:T(8,128)(2,1)} reshape(bf16[6,2,32,8,1,2304]{5,3,2,1,0,4:T(8,128)(2,1)} %bitcast.329) | data formatting | bytes 28311552 | tf_op jit(solution)/shard_map/reshape | solution.py:110
  383.5 27.9 %bitcast_convert_fusion.1 = bf16[6,32,256,256]{3,2,1,0:T(8,128)(2,1)} fusion(bf16[2,4,48,2,256,1,1,1]{4,2,1,3,0,7,6,5:T(8,128)(2,1)S(1)} %bitcast.350, bf16[2,2,48,256,1,1]{3,2,1,0,5,4:T(8,128)(2,1)S(1)} %bitcast.346, bf16[6,2,32,4,2,48,48]{6,5,4,3,2,1,0:T(8,128)(2,1)} %reshape.1119), kind=kOutput, calls=%fused_computation.16 | convolution fusion | flops 12101615616 | bytes 39813120 | tf_op jit(solution)/shard_map/cxtlmy,tlmz->cxyz/dot_general | solution.py:114
  422.0 36.4 %reshape.1120 = bf16[3,8,4,4,64,4,64]{6,5,4,3,2,1,0:T(4,128)(2,1)} reshape(bf16[3,32,256,256]{3,2,1,0:T(8,128)(2,1)} %slice.156) | data formatting | bytes 25165824 | tf_op jit(solution)/shard_map/reshape | solution.py:150
  458.3 22.6 %copy.227 = bf16[3,8,4,4,64,4,64]{6,4,1,5,3,2,0:T(8,128)(2,1)} copy(bf16[3,8,4,4,64,4,64]{6,5,4,3,2,1,0:T(4,128)(2,1)} %reshape.1120) | data formatting | bytes 25165824 | tf_op jit(solution)/shard_map/reshape | solution.py:150
  481.0 29.1 %reshape.1121 = bf16[192,32768]{1,0:T(8,128)(2,1)} reshape(bf16[3,4,4,4,8,64,64]{6,5,4,3,2,1,0:T(8,128)(2,1)} %bitcast.327) | data formatting | bytes 25165824 | tf_op jit(solution)/shard_map/reshape | solution.py:153
  510.1 27.8 %fusion.135 = f32[32768,512]{1,0:T(8,128)} fusion(bf16[192,32768]{1,0:T(8,128)(2,1)} %reshape.1121, bf16[512,192]{0,1:T(8,128)(2,1)S(1)} %copy-done), kind=kOutput, calls=%fused_computation.239 | convolution fusion | flops 6442450944 | bytes 79888384 | tf_op jit(solution)/shard_map/dot_general | solution.py:167
  537.9 46.2 %convert_reduce_fusion = (f32[512]{0:T(512)S(1)}, bf16[512,32768]{0,1:T(8,128)(2,1)}) fusion(f32[32768,512]{1,0:T(8,128)} %fusion.135, f32[512]{0:T(512)S(1)} %copy-done.31, bf16[192,32768]{1,0:T(8,128)(2,1)} %reshape.1117, bf16[192,512]{1,0:T(8,128)(2,1)S(1)} %copy-done.30), kind=kOutput, calls=%fused_computation.15 | convolution fusion | flops 6660554240 | bytes 113446912 | tf_op jit(solution)/shard_map/dot_general | solution.py:170
  585.0 25.6 %convolution_bitcast_fusion = f32[192,32768]{1,0:T(8,128)} fusion(bf16[512,32768]{0,1:T(8,128)(2,1)} %get-tuple-element.56, bf16[512,192]{0,1:T(8,128)(2,1)S(1)} %copy-done), kind=kOutput, calls=%fused_computation.18 | convolution fusion | flops 6442450944 | bytes 58916864 | tf_op jit(solution)/shard_map/dot_general | solution.py:175
  610.6 36.4 %reshape.1122 = f32[3,4,4,4,8,64,64]{6,5,4,3,2,1,0:T(8,128)} reshape(f32[192,32768]{1,0:T(8,128)} %convolution_bitcast_fusion) | data formatting | bytes 50331648 | tf_op jit(solution)/shard_map/reshape | solution.py:158
  647.0 55.7 %copy.226 = f32[3,4,4,4,8,64,64]{6,3,5,2,1,4,0:T(4,128)} copy(f32[3,4,4,4,8,64,64]{6,5,4,3,2,1,0:T(8,128)} %reshape.1122) | data formatting | bytes 50331648 | tf_op jit(solution)/shard_map/reshape | solution.py:158
  702.7 32.7 %fusion.132 = (f32[1,8,4,4,64,4,64]{6,5,4,3,2,1,0:T(4,128)}, f32[1,8,4,4,64,4,64]{6,5,4,3,2,1,0:T(4,128)}, f32[1,8,4,4,64,4,64]{6,5,4,3,2,1,0:T(4,128)}) fusion(f32[3,8,4,4,64,4,64]{6,5,4,3,2,1,0:T(4,128)} %bitcast.325), kind=kLoop, calls=%fused_computation.236 | loop fusion | bytes 50331648 | tf_op jit(solution)/shard_map/slice | solution.py:184
  834.6 19.8 %fusion.13 = bf16[2,2,48,6,32,256]{5,2,0,4,1,3:T(8,128)(2,1)} fusion(bf16[6,32,256,256]{3,2,1,0:T(8,128)(2,1)} %fusion.61, bf16[2,2,48,256,1,1]{3,2,1,0,5,4:T(8,128)(2,1)S(1)} %bitcast.347), kind=kOutput, calls=%fused_computation.27 | convolution fusion | flops 4831838208 | bytes 44138496 | tf_op jit(solution)/shard_map/cxyz,rlmz->crlmxy/dot_general | solution.py:134
  854.3 50.7 %fusion.7 = bf16[6,2,32,4,2,48,48]{6,5,2,4,0,3,1:T(8,128)(2,1)} fusion(bf16[2,2,48,6,32,256]{5,2,0,4,1,3:T(8,128)(2,1)} %fusion.13, bf16[2,256,2,4,48,1,1,1]{1,4,3,2,0,7,6,5:T(8,128)(2,1)S(1)} %bitcast.348), kind=kOutput, calls=%fused_computation.19 | convolution fusion | flops 7254835200 | bytes 33423360 | tf_op jit(solution)/shard_map/crlmxy,rysja->csxjlam/dot_general | solution.py:137
  905.1 26.0 %copy.189 = bf16[6,2,32,4,2,48,48]{6,5,2,1,0,4,3:T(8,128)(2,1)} copy(bf16[6,2,32,4,2,48,48]{6,5,2,4,0,3,1:T(8,128)(2,1)} %fusion.7) | data formatting | bytes 28311552 | tf_op jit(solution)/shard_map/reshape | solution.py:140
  931.1 51.2 %reshape.1172 = bf16[6,2,32,8,2304]{4,2,1,0,3:T(8,128)(2,1)} reshape(bf16[6,2,32,4,2,48,48]{6,5,2,1,0,4,3:T(8,128)(2,1)} %copy.189) | data formatting | bytes 28311552 | tf_op jit(solution)/shard_map/reshape | solution.py:140
  987.8 18.3 %fusion.136 = f32[512,192]{1,0:T(8,128)} fusion(bf16[512,32768]{0,1:T(8,128)(2,1)} %get-tuple-element.56, bf16[192,32768]{1,0:T(8,128)(2,1)} %reshape.1121), kind=kOutput, calls=%fused_computation.240 | convolution fusion | flops 6442450944 | bytes 46530560 | tf_op jit(solution)/shard_map/dot_general | solution.py:172
  1006.2 31.2 %fusion.78 = f32[192,512]{0,1:T(8,128)} fusion(bf16[192,32768]{1,0:T(8,128)(2,1)} %reshape.1117, f32[32768,512]{1,0:T(8,128)} %fusion.135, f32[512]{0:T(512)S(1)} %copy-done.32), kind=kOutput, calls=%fused_computation.136 | convolution fusion | flops 6543212544 | bytes 80087040 | tf_op jit(solution)/shard_map/dot_general | solution.py:173
  1038.8 108.1 %all-to-all-done.2 = bf16[6,2,32,8,2304]{4,2,1,0,3:T(8,128)(2,1)} async-done(((bf16[6,2,32,8,2304]{4,2,1,0,3:T(8,128)(2,1)}), bf16[6,2,32,8,2304]{4,2,1,0,3:T(8,128)(2,1)}, u32[]{:S(2)}, u32[]{:S(2)}) %all-to-all-start.2) | async-done | bytes 14155808 | tf_op jit(solution)/shard_map/all_to_all | solution.py:141
  (176 shorter events, 385.5 us)
Async XLA Ops:
  7.2 502.9 %copy-start = (bf16[512,192]{0,1:T(8,128)(2,1)S(1)}, bf16[512,192]{0,1:T(8,128)(2,1)}, u32[]{:S(2)}) copy-start(bf16[512,192]{0,1:T(8,128)(2,1)} %param.7) | copy-start | bytes 589828
  8.3 12.5 copy-start.27
  8.8 67.1 %copy-start.19 = (f32[48]{0:T(128)}, f32[48]{0:T(128)S(1)}, u32[]{:S(2)}) copy-start(f32[48]{0:T(128)S(1)} %get-tuple-element.65) | copy-start | bytes 580
  70.0 84.8 %all-to-all-start = ((bf16[3,2,256,1,2304]{4,1,3,0,2:T(2,128)(2,1)}), bf16[3,2,256,1,2304]{4,1,3,0,2:T(2,128)(2,1)}, u32[]{:S(2)}, u32[]{:S(2)}) async-start(bf16[3,2,256,1,2304]{4,1,3,0,2:T(2,128)(2,1)} %copy.130), calls=%async_computation | async-start | bytes 14155776 | tf_op jit(solution)/shard_map/all_to_all | solution.py:109
  154.8 160.5 %all-to-all-start.1 = ((bf16[6,2,256,1,2304]{4,1,3,0,2:T(2,128)(2,1)}), bf16[6,2,256,1,2304]{4,1,3,0,2:T(2,128)(2,1)}, u32[]{:S(2)}, u32[]{:S(2)}) async-start(bf16[6,2,256,1,2304]{4,1,3,0,2:T(2,128)(2,1)} %copy.136), calls=%async_computation.1 | async-start | bytes 28311552 | tf_op jit(solution)/shard_map/all_to_all | solution.py:109
  160.3 877.1 %reduce-scatter.10.cloned.1.call-start = ((), (), s32[]{:S(2)}) async-start(), calls=%async_computation.8 | async-start | bytes 294912
  162.4 221.1 %copy-start.10 = (bf16[2,96,256]{2,1,0:T(8,128)(2,1)}, bf16[2,96,256]{2,1,0:T(8,128)(2,1)S(1)}, u32[]{:S(2)}) copy-start(bf16[2,96,256]{2,1,0:T(8,128)(2,1)S(1)} %copy.126) | copy-start | bytes 294916
  510.1 27.8 %copy-start.30 = (bf16[192,512]{1,0:T(8,128)(2,1)S(1)}, bf16[192,512]{1,0:T(8,128)(2,1)}, u32[]{:S(2)}) copy-start(bf16[192,512]{1,0:T(8,128)(2,1)} %param.9) | copy-start | bytes 589828
  510.1 27.8 %copy-start.31 = (f32[512]{0:T(512)S(1)}, f32[512]{0:T(512)}, u32[]{:S(2)}) copy-start(f32[512]{0:T(512)} %param.8) | copy-start | bytes 6148
  783.0 25.0 %slice-start = ((s8[12582912]{0:T(1024)(128)(4,1)}), s8[4194304]{0:T(1024)(128)(4,1)S(1)}, s32[]{:S(2)}) async-start(s8[12582912]{0:T(1024)(128)(4,1)} %bitcast.323), calls=%async_computation.9 | async-start | bytes 8388608
  783.0 25.0 %slice-start.1 = ((s8[12582912]{0:T(1024)(128)(4,1)}), s8[4194304]{0:T(1024)(128)(4,1)S(1)}, s32[]{:S(2)}) async-start(s8[12582912]{0:T(1024)(128)(4,1)} %bitcast.323), calls=%async_computation.10 | async-start | bytes 8388608
  783.0 25.0 %slice-start.7 = ((s8[8388608]{0:T(1024)(128)(4,1)}), s8[4194304]{0:T(1024)(128)(4,1)S(1)}, s32[]{:S(2)}) async-start(s8[8388608]{0:T(1024)(128)(4,1)} %bitcast.335), calls=%async_computation.16 | async-start | bytes 8388608
  795.3 12.6 slice-start.2
  795.3 12.6 slice-start.8
  834.6 19.8 %copy-start.12 = (bf16[2,256,2,192]{1,3,2,0:T(8,128)(2,1)S(1)}, bf16[2,256,2,192]{1,3,2,0:T(8,128)(2,1)}, u32[]{:S(2)}) copy-start(bf16[2,256,2,192]{1,3,2,0:T(8,128)(2,1)} %copy.124) | copy-start | bytes 1179652
  982.2 164.7 %all-to-all-start.2 = ((bf16[6,2,32,8,2304]{4,2,1,0,3:T(8,128)(2,1)}), bf16[6,2,32,8,2304]{4,2,1,0,3:T(8,128)(2,1)}, u32[]{:S(2)}, u32[]{:S(2)}) async-start(bf16[6,2,32,8,2304]{4,2,1,0,3:T(8,128)(2,1)} %reshape.1172), calls=%async_computation.2 | async-start | bytes 28311552 | tf_op jit(solution)/shard_map/all_to_all | solution.py:141
  987.7 18.4 %copy-start.32 = (f32[512]{0:T(512)S(1)}, f32[512]{0:T(512)}, u32[]{:S(2)}) copy-start(f32[512]{0:T(512)} %param.8) | copy-start | bytes 6148
  987.8 274.4 %reduce-scatter.6.cloned.1.call-start = ((), (), s32[]{:S(2)}) async-start(), calls=%async_computation.6 | async-start | bytes 589824 | tf_op jit(solution)/shard_map/reduce_scatter | solution.py:212
  1006.1 256.0 %reduce-scatter.8.cloned.1.call-start = ((), (), s32[]{:S(2)}) async-start(), calls=%async_computation.7 | async-start | bytes 589824 | tf_op jit(solution)/shard_map/reduce_scatter | solution.py:213
  1146.9 10.6 copy-start.9
  1193.8 15.2 %copy-start.20 = (f32[48]{0:T(128)S(1)}, f32[48]{0:T(128)}, u32[]{:S(2)}) copy-start(f32[48]{0:T(128)} %copy-done.19) | copy-start | bytes 580
  1193.8 15.2 %copy-start.23 = (f32[48]{0:T(128)S(1)}, f32[48]{0:T(128)}, u32[]{:S(2)}) copy-start(f32[48]{0:T(128)} %get-tuple-element.66) | copy-start | bytes 580
  1193.8 15.2 %copy-start.26 = (f32[256]{0:T(256)S(1)}, f32[256]{0:T(256)}, u32[]{:S(2)}) copy-start(f32[256]{0:T(256)} %fusion.120) | copy-start | bytes 3076
  1247.3 14.8 %copy-start.1 = (bf16[512,192]{0,1:T(8,128)(2,1)S(1)}, bf16[512,192]{0,1:T(8,128)(2,1)}, u32[]{:S(2)}) copy-start(bf16[512,192]{0,1:T(8,128)(2,1)} %param.7) | copy-start | bytes 589828
  (24 other events, 162.1 us)
Sparse Core Ops, SparseCore 0:
  585.2 35.3 reduce-scatter.9
  1006.2 38.0 reduce-scatter.5
  1047.9 73.2 reduce-scatter.7
where the time goes:
time: 1290 us; the launch traced here: 1270 us
  local copies, waits for them, and re-layouts  680 us (53%)
  matrix products  307 us (24%)
  other arithmetic  136 us (11%)
  waiting for transfers between devices  114 us (9%)
  starting transfers between devices  17 us (1%)
  between operations  14.8 us (1%)
    reshape x4, local copies, waits for them, and re-layouts, to_boxes(): field.reshape(channels, span_x // PATCH, PATCH, PATCH, span_y // PATCH, P...  118 us
    all_to_all x1, waiting for transfers between devices, to_spectral(): lax.all_to_all(along_y, ('px', 'py'), split_axis=3, concat_axis=2, tiled=...  108 us
    reshape x2, local copies, waits for them, and re-layouts, from_boxes(): box_values.reshape(channels, PATCH, PATCH, PATCH, span_x // PATCH, span_y...  92 us
    reshape x2, local copies, waits for them, and re-layouts, to_physical(): moved.reshape(moved.shape[0], 2, moved.shape[2], parts_x, parts_y, width_...  85.1 us
    reshape x2, local copies, waits for them, and re-layouts, to_spectral(): along_y.reshape(channels, 2, span_x, parts_x * parts_y, width_y * width_z)  77.1 us
    reshape x2, local copies, waits for them, and re-layouts, to_boxes(): tiles.transpose(0, 2, 3, 5, 1, 4, 6).reshape(channels * PATCH ** 3, -1)  58.2 us
    dot_general x1, matrix products, to_spectral(): jnp.einsum('crlmxy,rysja->csxjlam', along_z, y_table, preferred_element_t...  50.7 us
    reshape x2, local copies, waits for them, and re-layouts, to_physical(): along_x = along_x.reshape(channels, 2, length, 1, width_y * width_z)  50.2 us
  transfers between devices with their start and end apart: 6, of which 3 were waited for; matrix products, arithmetic and copies ran while one was open for 62% of the time, Pallas kernels for 0%

commit v1 on v0

--- a/solution.py
+++ b/solution.py
@@ -172,18 +172,16 @@
     grad_in = jnp.dot(pre_adj, features.T, preferred_element_type=jnp.float32)
     grad_out = FORCING * jnp.dot(adjoints, hidden.T, preferred_element_type=jnp.float32)
     grad_bias = jnp.sum(pre_adj.astype(jnp.float32), axis=1)[None, :]
-    feat_adj = jnp.dot(w_in.T, pre_adj, preferred_element_type=jnp.float32)
-    return (from_boxes(feat_adj, velocity.shape), grad_in, grad_out, grad_bias)
-
-
-def pointwise(feat_adj, velocity, vorticity, force_adj):
-    vel_list = [velocity[slot].astype(jnp.float32) for slot in range(3)]
-    vort_list = [vorticity[slot].astype(jnp.float32) for slot in range(3)]
-    force_list = [force_adj[slot].astype(jnp.float32) for slot in range(3)]
-    turned = cross(vort_list, force_list)
-    vel_adj = jnp.stack([feat_adj[slot] + turned[slot] for slot in range(3)]).astype(jnp.bfloat16)
-    vort_adj = jnp.stack(cross(force_list, vel_list)).astype(jnp.bfloat16)
-    return (vel_adj, vort_adj)
+    feat_adj = jnp.dot(w_in.T, pre_adj, preferred_element_type=jnp.float32).astype(jnp.bfloat16)
+    feat_adj = lax.optimization_barrier(from_boxes(feat_adj, velocity.shape))
+    return (feat_adj, grad_in, grad_out, grad_bias)
+
+
+def field_cross(former, latter):
+    return cross(
+        [former[slot].astype(jnp.float32) for slot in range(3)],
+        [latter[slot].astype(jnp.float32) for slot in range(3)],
+    )
 
 
 def shards(state, cotangent, w_in, b_in, w_out):
@@ -195,18 +193,19 @@
     kz_ids = lax.axis_index("py") * width_z + jnp.arange(width_z, dtype=jnp.int32)
     waves, retained, damping, weight, square = factors(ky_ids, kz_ids, length, ky_count)
     kept = retained * state
-    spectra = weight * jnp.concatenate([kept, curl_modes(waves, kept)], axis=0)
     force_spec = TIME_STEP * retained * project(waves, square, damping * cotangent)
-    fields = to_physical(spectra)
-    velocity, vorticity = (fields[:3], fields[3:])
+    modes = width_z * lax.axis_size("py")
     force_adj = to_physical(force_spec)
+    velocity = to_physical(weight * kept)
+    vorticity = to_physical(weight * curl_modes(waves, kept))
+    vort_adj = jnp.stack(field_cross(force_adj, velocity)).astype(jnp.bfloat16)
+    spec_vort = to_spectral(vort_adj, ky_count, modes)
     feat_adj, grad_in, grad_out, grad_bias = closure_terms(velocity, force_adj, w_in, b_in, w_out)
-    vel_adj, vort_adj = pointwise(feat_adj, velocity, vorticity, force_adj)
-    spectral = to_spectral(
-        jnp.concatenate([vel_adj, vort_adj], axis=0), ky_count, width_z * lax.axis_size("py")
-    )
+    turned = field_cross(vorticity, force_adj)
+    vel_adj = jnp.stack([feat_adj[slot].astype(jnp.float32) + turned[slot] for slot in range(3)])
+    spec_vel = to_spectral(vel_adj.astype(jnp.bfloat16), ky_count, modes)
     state_grad = damping * cotangent + weight * retained * (
-        spectral[:3] + curl_modes(waves, spectral[3:])
+        spec_vel + curl_modes(waves, spec_vort)
     )
     grad_in, grad_out, grad_bias = (
         lax.psum_scatter(grad_in, ("px", "py"), scatter_dimension=0, tiled=True),

time: 1290 us -> 1150 us (0.89)
  waiting for transfers between devices: 114 us -> 46.9 us
  local copies, waits for them, and re-layouts: 680 us -> 618 us
  other arithmetic: 136 us -> 115 us
  starting transfers between devices: 17 us -> 36 us
    all_to_all x1 -> x2, waiting for transfers between devices: 108 us -> 13.9 us  [to_spectral(): lax.all_to_all(along_y, ('px', 'py'), split_axis=3, concat_axis=2, tiled=...]
    slice x5 -> x0, local copies, waits for them, and re-layouts: 92 us -> none  [the longest x2 33.3 us: shards(): spectral[3:]]
    squeeze x3 -> x0, local copies, waits for them, and re-layouts: 47.6 us -> none  [pointwise(): feat_adj[slot] + turned[slot]]
    unnamed x8 -> x2, other arithmetic: 45 us -> 0.01 us
    reshape x0 -> x1, local copies, waits for them, and re-layouts: none -> 35.7 us  [from_boxes(): return tiles.transpose(0, 4, 1, 2, 5, 3, 6).reshape(layout)]
    reshape x2, local copies, waits for them, and re-layouts: 92 us -> 59.9 us  [from_boxes(): box_values.reshape(channels, PATCH, PATCH, PATCH, span_x // PATCH, span_y...]
    transpose x0 -> x2, local copies, waits for them, and re-layouts: none -> 30.7 us  [to_spectral(): jnp.einsum('csxp,sxtn->ctpn', flat, forward, preferred_element_type=jnp.f...]
    another operation x4 -> x6, other arithmetic: 3.95 us -> 33.8 us
  transfers between devices with their start and end apart: 6 -> 8, of which waited for: 3 -> 2; matrix products, arithmetic and copies ran while one was open for 62% -> 85% of each run, Pallas kernels for 0% -> 0%
where the time goes in v1:
time: 1150 us; the launch traced here: 1130 us
  local copies, waits for them, and re-layouts  618 us (54%)
  matrix products  297 us (26%)
  other arithmetic  115 us (10%)
  waiting for transfers between devices  46.9 us (4%)
  starting transfers between devices  36 us (3%)
  between operations  14.9 us (1%)
    reshape x4, local copies, waits for them, and re-layouts, to_boxes(): field.reshape(channels, span_x // PATCH, PATCH, PATCH, span_y // PATCH, P...  118 us
    reshape x4, local copies, waits for them, and re-layouts, to_spectral(): along_y.reshape(channels, 2, span_x, parts_x * parts_y, width_y * width_z)  88.9 us
    reshape x3, local copies, waits for them, and re-layouts, to_physical(): moved.reshape(moved.shape[0], 2, moved.shape[2], parts_x, parts_y, width_...  87.1 us
    reshape x3, local copies, waits for them, and re-layouts, to_physical(): along_x = along_x.reshape(channels, 2, length, 1, width_y * width_z)  75.2 us
    reshape x2, local copies, waits for them, and re-layouts, from_boxes(): box_values.reshape(channels, PATCH, PATCH, PATCH, span_x // PATCH, span_y...  59.9 us
    reshape x2, local copies, waits for them, and re-layouts, to_boxes(): tiles.transpose(0, 2, 3, 5, 1, 4, 6).reshape(channels * PATCH ** 3, -1)  58.2 us
    dot_general x2, matrix products, to_spectral(): jnp.einsum('crlmxy,rysja->csxjlam', along_z, y_table, preferred_element_t...  55.5 us
    dot_general x3, matrix products, to_physical(): jnp.einsum('cxtlmy,tlmz->cxyz', along_y, z_table, preferred_element_type=...  48.8 us
  transfers between devices with their start and end apart: 8, of which 2 were waited for; matrix products, arithmetic and copies ran while one was open for 85% of the time, Pallas kernels for 0%

profile of v1, /device:TPU:0, one launch (start us, length us, event | category | flops | bytes accessed | tf_op | source)
XLA Modules:
  0.0 1128.6 jit_solution(6317094853116231177)
XLA Ops:
  46.3 23.6 %copy.174 = bf16[3,2,256,1,2304]{4,1,3,0,2:T(2,128)(2,1)} copy(bf16[3,2,256,1,2304]{4,2,0,1,3:T(8,128)(2,1)S(1)} %fusion.75) | data formatting | bytes 14155776 | tf_op jit(solution)/shard_map/reshape | solution.py:108
  105.6 27.6 %copy.180 = bf16[3,2,256,1,2304]{4,1,3,0,2:T(2,128)(2,1)} copy(bf16[3,2,256,1,2304]{4,2,0,1,3:T(8,128)(2,1)} %fusion.74) | data formatting | bytes 14155776 | tf_op jit(solution)/shard_map/reshape | solution.py:108
  133.2 33.0 %all-to-all-done = bf16[3,2,256,1,2304]{4,1,3,0,2:T(2,128)(2,1)} async-done(((bf16[3,2,256,1,2304]{4,1,3,0,2:T(2,128)(2,1)}), bf16[3,2,256,1,2304]{4,1,3,0,2:T(2,128)(2,1)}, u32[]{:S(2)}, u32[]{:S(2)}) %all-to-all-start) | async-done | bytes 7077920 | tf_op jit(solution)/shard_map/all_to_all | solution.py:109
  204.4 24.0 %copy.187 = bf16[3,2,256,1,2304]{4,1,3,0,2:T(2,128)(2,1)} copy(bf16[3,2,256,1,2304]{4,2,0,1,3:T(8,128)(2,1)S(1)} %fusion.78) | data formatting | bytes 14155776 | tf_op jit(solution)/shard_map/reshape | solution.py:108
  240.1 28.9 %reshape.1131 = bf16[3,2,32,4,2,48,48]{6,5,4,3,2,1,0:T(8,128)(2,1)} reshape(bf16[3,2,32,8,1,2304]{5,3,2,1,0,4:T(8,128)(2,1)} %bitcast.414) | data formatting | bytes 14155776 | tf_op jit(solution)/shard_map/reshape | solution.py:110
  283.7 29.0 %reshape.1136 = bf16[3,2,32,4,2,48,48]{6,5,4,3,2,1,0:T(8,128)(2,1)} reshape(bf16[3,2,32,8,1,2304]{5,3,2,1,0,4:T(8,128)(2,1)} %bitcast.415) | data formatting | bytes 14155776 | tf_op jit(solution)/shard_map/reshape | solution.py:110
  328.9 36.2 %reshape.1137 = bf16[3,8,4,4,64,4,64]{6,5,4,3,2,1,0:T(4,128)(2,1)} reshape(bf16[3,32,256,256]{3,2,1,0:T(8,128)(2,1)} %bitcast_convert_fusion.3) | data formatting | bytes 25165824 | tf_op jit(solution)/shard_map/reshape | solution.py:150
  381.4 36.2 %reshape.1132 = bf16[3,8,4,4,64,4,64]{6,5,4,3,2,1,0:T(4,128)(2,1)} reshape(bf16[3,32,256,256]{3,2,1,0:T(8,128)(2,1)} %bitcast_convert_fusion.4) | data formatting | bytes 25165824 | tf_op jit(solution)/shard_map/reshape | solution.py:150
  469.1 26.4 %reshape.1212 = bf16[3,2,32,8,2304]{4,2,1,0,3:T(8,128)(2,1)} reshape(bf16[3,2,32,4,2,48,48]{6,5,2,1,0,4,3:T(8,128)(2,1)} %copy.270) | data formatting | bytes 14155776 | tf_op jit(solution)/shard_map/reshape | solution.py:140
  495.5 22.6 %copy.327 = bf16[3,8,4,4,64,4,64]{6,4,1,5,3,2,0:T(8,128)(2,1)} copy(bf16[3,8,4,4,64,4,64]{6,5,4,3,2,1,0:T(4,128)(2,1)} %reshape.1137) | data formatting | bytes 25165824 | tf_op jit(solution)/shard_map/reshape | solution.py:150
  518.2 29.1 %reshape.1138 = bf16[192,32768]{1,0:T(8,128)(2,1)} reshape(bf16[3,4,4,4,8,64,64]{6,5,4,3,2,1,0:T(8,128)(2,1)} %bitcast.405) | data formatting | bytes 25165824 | tf_op jit(solution)/shard_map/reshape | solution.py:153
  562.0 29.2 %reshape.1142 = bf16[3,2,32,4,2,48,48]{6,5,4,3,2,1,0:T(8,128)(2,1)} reshape(bf16[3,2,32,8,1,2304]{5,3,2,1,0,4:T(8,128)(2,1)} %bitcast.416) | data formatting | bytes 14155776 | tf_op jit(solution)/shard_map/reshape | solution.py:110
  607.3 22.6 %copy.328 = bf16[3,8,4,4,64,4,64]{6,4,1,5,3,2,0:T(8,128)(2,1)} copy(bf16[3,8,4,4,64,4,64]{6,5,4,3,2,1,0:T(4,128)(2,1)} %reshape.1132) | data formatting | bytes 25165824 | tf_op jit(solution)/shard_map/reshape | solution.py:150
  629.9 29.1 %reshape.1133 = bf16[192,32768]{1,0:T(8,128)(2,1)} reshape(bf16[3,4,4,4,8,64,64]{6,5,4,3,2,1,0:T(8,128)(2,1)} %bitcast.406) | data formatting | bytes 25165824 | tf_op jit(solution)/shard_map/reshape | solution.py:153
  659.0 27.8 %fusion.156 = f32[32768,512]{1,0:T(8,128)} fusion(bf16[192,32768]{1,0:T(8,128)(2,1)} %reshape.1138, bf16[512,192]{0,1:T(8,128)(2,1)S(1)} %copy-done), kind=kOutput, calls=%fused_computation.263 | convolution fusion | flops 6442450944 | bytes 79888384 | tf_op jit(solution)/shard_map/dot_general | solution.py:167
  686.8 46.9 %convert_reduce_fusion = (f32[512]{0:T(512)S(1)}, bf16[512,32768]{0,1:T(8,128)(2,1)}) fusion(f32[32768,512]{1,0:T(8,128)} %fusion.156, f32[512]{0:T(512)S(1)} %copy-done.32, bf16[192,32768]{1,0:T(8,128)(2,1)} %reshape.1133, bf16[192,512]{1,0:T(8,128)(2,1)S(1)} %copy-done.31), kind=kOutput, calls=%fused_computation.14 | convolution fusion | flops 6660554240 | bytes 113446912 | tf_op jit(solution)/shard_map/dot_general | solution.py:170
  734.7 21.2 %fusion.7 = bf16[192,32768]{1,0:T(8,128)(2,1)} fusion(bf16[512,32768]{0,1:T(8,128)(2,1)} %get-tuple-element.59, bf16[512,192]{0,1:T(8,128)(2,1)S(1)} %copy-done), kind=kOutput, calls=%fused_computation.16 | convolution fusion | flops 6448742400 | bytes 46333952 | tf_op jit(solution)/shard_map/dot_general | solution.py:175
  755.8 30.9 %reshape.1139 = bf16[3,4,4,4,8,64,64]{6,5,4,3,2,1,0:T(8,128)(2,1)} reshape(bf16[192,32768]{1,0:T(8,128)(2,1)} %fusion.7) | data formatting | bytes 25165824 | tf_op jit(solution)/shard_map/reshape | solution.py:158
  786.7 29.0 %copy.326 = bf16[3,4,4,4,8,64,64]{6,3,5,2,1,4,0:T(4,128)(2,1)} copy(bf16[3,4,4,4,8,64,64]{6,5,4,3,2,1,0:T(8,128)(2,1)} %reshape.1139) | data formatting | bytes 25165824 | tf_op jit(solution)/shard_map/reshape | solution.py:158
  815.7 35.7 %reshape.1140 = bf16[3,32,256,256]{3,2,1,0:T(8,128)(2,1)} reshape(bf16[3,8,4,4,64,4,64]{6,5,4,3,2,1,0:T(4,128)(2,1)} %bitcast.407) | data formatting | bytes 25165824 | tf_op jit(solution)/shard_map/reshape | solution.py:161
  851.4 18.5 %fusion.44 = (bf16[1,32,256,256]{3,2,1,0:T(8,128)(2,1)}, bf16[1,32,256,256]{3,2,1,0:T(8,128)(2,1)}, bf16[1,32,256,256]{3,2,1,0:T(8,128)(2,1)}) fusion(bf16[3,32,256,256]{3,2,1,0:T(8,128)(2,1)} %reshape.1140, bf16[3,32,256,256]{3,2,1,0:T(8,128)(2,1)} %bitcast_convert_fusion.2, bf16[3,32,256,256]{3,2,1,0:T(8,128)(2,1)} %bitcast_convert_fusion.4), kind=kLoop, calls=%fused_computation.81 | loop fusion | flops 50331648 | bytes 50331648 | tf_op jit(solution)/shard_map/convert.3
  879.6 39.9 %fusion.10 = bf16[3,2,32,4,2,48,48]{6,5,2,4,0,3,1:T(8,128)(2,1)} fusion(bf16[2,2,48,3,32,256]{5,2,0,4,1,3:T(8,128)(2,1)} %fusion.22, bf16[2,256,2,4,48,1,1,1]{1,4,3,2,0,7,6,5:T(8,128)(2,1)S(1)} %bitcast.428), kind=kOutput, calls=%fused_computation.26 | convolution fusion | flops 3627417600 | bytes 16908288 | tf_op jit(solution)/shard_map/crlmxy,rysja->csxjlam/dot_general | solution.py:137
  953.0 26.2 %reshape.1211 = bf16[3,2,32,8,2304]{4,2,1,0,3:T(8,128)(2,1)} reshape(bf16[3,2,32,4,2,48,48]{6,5,2,1,0,4,3:T(8,128)(2,1)} %copy.263) | data formatting | bytes 14155776 | tf_op jit(solution)/shard_map/reshape | solution.py:140
  984.2 31.2 %fusion.92 = f32[192,512]{0,1:T(8,128)} fusion(bf16[192,32768]{1,0:T(8,128)(2,1)} %reshape.1133, f32[32768,512]{1,0:T(8,128)} %fusion.156, f32[512]{0:T(512)S(1)} %copy-done.32), kind=kOutput, calls=%fused_computation.154 | convolution fusion | flops 6543212544 | bytes 80087040 | tf_op jit(solution)/shard_map/dot_general | solution.py:173
  (177 shorter events, 409.0 us)
Async XLA Ops:
  7.2 651.8 %copy-start = (bf16[512,192]{0,1:T(8,128)(2,1)S(1)}, bf16[512,192]{0,1:T(8,128)(2,1)}, u32[]{:S(2)}) copy-start(bf16[512,192]{0,1:T(8,128)(2,1)} %param.7) | copy-start | bytes 589828
  8.9 162.3 %copy-start.20 = (f32[48]{0:T(128)}, f32[48]{0:T(128)S(1)}, u32[]{:S(2)}) copy-start(f32[48]{0:T(128)S(1)} %get-tuple-element.68) | copy-start | bytes 580
  69.9 16.6 %copy-start.17 = (pred[48,256]{1,0:T(8,128)(4,1)S(1)}, pred[48,256]{1,0:T(8,128)(4,1)}, u32[]{:S(2)}) copy-start(pred[48,256]{1,0:T(8,128)(4,1)} %copy-done.16) | copy-start | bytes 36868
  69.9 16.6 %copy-start.30 = (pred[48]{0:T(512)(128)(4,1)S(1)}, pred[48]{0:T(512)(128)(4,1)}, u32[]{:S(2)}) copy-start(pred[48]{0:T(512)(128)(4,1)} %copy-done.29) | copy-start | bytes 148
  69.9 17.0 %copy-start.28 = (f32[48]{0:T(128)S(1)}, f32[48]{0:T(128)}, u32[]{:S(2)}) copy-start(f32[48]{0:T(128)} %get-tuple-element.60) | copy-start | bytes 580
  69.9 96.3 %all-to-all-start = ((bf16[3,2,256,1,2304]{4,1,3,0,2:T(2,128)(2,1)}), bf16[3,2,256,1,2304]{4,1,3,0,2:T(2,128)(2,1)}, u32[]{:S(2)}, u32[]{:S(2)}) async-start(bf16[3,2,256,1,2304]{4,1,3,0,2:T(2,128)(2,1)} %copy.174), calls=%async_computation | async-start | bytes 14155776 | tf_op jit(solution)/shard_map/all_to_all | solution.py:109
  133.2 38.1 %copy-start.23 = (f32[48]{0:T(128)S(1)}, f32[48]{0:T(128)}, u32[]{:S(2)}) copy-start(f32[48]{0:T(128)} %get-tuple-element.69) | copy-start | bytes 580
  166.2 102.8 %all-to-all-start.1 = ((bf16[3,2,256,1,2304]{4,1,3,0,2:T(2,128)(2,1)}), bf16[3,2,256,1,2304]{4,1,3,0,2:T(2,128)(2,1)}, u32[]{:S(2)}, u32[]{:S(2)}) async-start(bf16[3,2,256,1,2304]{4,1,3,0,2:T(2,128)(2,1)} %copy.180), calls=%async_computation.1 | async-start | bytes 14155776 | tf_op jit(solution)/shard_map/all_to_all | solution.py:109
  181.0 184.1 %copy-start.10 = (bf16[2,192,2,256]{3,1,2,0:T(8,128)(2,1)}, bf16[2,192,2,256]{3,1,2,0:T(8,128)(2,1)S(1)}, u32[]{:S(2)}) copy-start(bf16[2,192,2,256]{3,1,2,0:T(8,128)(2,1)S(1)} %copy.172) | copy-start | bytes 1179652
  269.0 278.2 %all-to-all-start.2 = ((bf16[3,2,256,1,2304]{4,1,3,0,2:T(2,128)(2,1)}), bf16[3,2,256,1,2304]{4,1,3,0,2:T(2,128)(2,1)}, u32[]{:S(2)}, u32[]{:S(2)}) async-start(bf16[3,2,256,1,2304]{4,1,3,0,2:T(2,128)(2,1)} %copy.187), calls=%async_computation.2 | async-start | bytes 14155776 | tf_op jit(solution)/shard_map/all_to_all | solution.py:109
  283.7 29.0 %copy-start.18 = (bf16[2,96,256]{2,1,0:T(8,128)(2,1)S(1)}, bf16[2,96,256]{2,1,0:T(8,128)(2,1)}, u32[]{:S(2)}) copy-start(bf16[2,96,256]{2,1,0:T(8,128)(2,1)} %copy.170) | copy-start | bytes 294916
  547.3 432.0 %all-to-all-start.4 = ((bf16[3,2,32,8,2304]{4,2,1,0,3:T(8,128)(2,1)}), bf16[3,2,32,8,2304]{4,2,1,0,3:T(8,128)(2,1)}, u32[]{:S(2)}, u32[]{:S(2)}) async-start(bf16[3,2,32,8,2304]{4,2,1,0,3:T(8,128)(2,1)} %reshape.1212), calls=%async_computation.4 | async-start | bytes 14155776 | tf_op jit(solution)/shard_map/all_to_all | solution.py:141
  552.1 463.4 %reduce-scatter.10.cloned.1.call-start = ((), (), s32[]{:S(2)}) async-start(), calls=%async_computation.10 | async-start | bytes 294912
  562.0 29.2 %copy-start.11 = (bf16[2,192,2,256]{3,1,2,0:T(8,128)(2,1)S(1)}, bf16[2,192,2,256]{3,1,2,0:T(8,128)(2,1)}, u32[]{:S(2)}) copy-start(bf16[2,192,2,256]{3,1,2,0:T(8,128)(2,1)} %copy-done.10) | copy-start | bytes 1179652
  659.0 27.8 %copy-start.31 = (bf16[192,512]{1,0:T(8,128)(2,1)S(1)}, bf16[192,512]{1,0:T(8,128)(2,1)}, u32[]{:S(2)}) copy-start(bf16[192,512]{1,0:T(8,128)(2,1)} %param.9) | copy-start | bytes 589828
  659.0 27.8 %copy-start.32 = (f32[512]{0:T(512)S(1)}, f32[512]{0:T(512)}, u32[]{:S(2)}) copy-start(f32[512]{0:T(512)} %param.8) | copy-start | bytes 6148
  734.6 387.0 %reduce-scatter.6.cloned.1.call-start = ((), (), s32[]{:S(2)}) async-start(), calls=%async_computation.8 | async-start | bytes 589824 | tf_op jit(solution)/shard_map/reduce_scatter | solution.py:211
  851.4 18.6 %copy-start.19 = (bf16[2,96,256]{2,1,0:T(8,128)(2,1)S(1)}, bf16[2,96,256]{2,1,0:T(8,128)(2,1)}, u32[]{:S(2)}) copy-start(bf16[2,96,256]{2,1,0:T(8,128)(2,1)} %copy.170) | copy-start | bytes 294916
  870.0 49.5 %slice-start.4 = ((s8[12582912]{0:T(1024)(128)(4,1)}), s8[4194304]{0:T(1024)(128)(4,1)S(1)}, s32[]{:S(2)}) async-start(s8[12582912]{0:T(1024)(128)(4,1)} %bitcast.412), calls=%async_computation.15 | async-start | bytes 8388608
  870.0 49.5 %slice-start.5 = ((s8[12582912]{0:T(1024)(128)(4,1)}), s8[4194304]{0:T(1024)(128)(4,1)S(1)}, s32[]{:S(2)}) async-start(s8[12582912]{0:T(1024)(128)(4,1)} %bitcast.412), calls=%async_computation.16 | async-start | bytes 8388608
  879.6 39.9 %slice-start.6 = ((s8[12582912]{0:T(1024)(128)(4,1)}), s8[4194304]{0:T(1024)(128)(4,1)S(1)}, s32[]{:S(2)}) async-start(s8[12582912]{0:T(1024)(128)(4,1)} %bitcast.412), calls=%async_computation.17 | async-start | bytes 8388608
  979.3 88.2 %all-to-all-start.3 = ((bf16[3,2,32,8,2304]{4,2,1,0,3:T(8,128)(2,1)}), bf16[3,2,32,8,2304]{4,2,1,0,3:T(8,128)(2,1)}, u32[]{:S(2)}, u32[]{:S(2)}) async-start(bf16[3,2,32,8,2304]{4,2,1,0,3:T(8,128)(2,1)} %reshape.1211), calls=%async_computation.3 | async-start | bytes 14155776 | tf_op jit(solution)/shard_map/all_to_all | solution.py:141
  984.2 137.4 %reduce-scatter.8.cloned.1.call-start = ((), (), s32[]{:S(2)}) async-start(), calls=%async_computation.9 | async-start | bytes 589824 | tf_op jit(solution)/shard_map/reduce_scatter | solution.py:212
  1027.9 15.3 %copy-start.27 = (f32[256]{0:T(256)S(1)}, f32[256]{0:T(256)}, u32[]{:S(2)}) copy-start(f32[256]{0:T(256)} %fusion.140) | copy-start | bytes 3076
  (24 other events, 186.7 us)
Sparse Core Ops, SparseCore 0:
  734.7 35.8 reduce-scatter.9
  979.4 41.3 reduce-scatter.5
  1024.5 36.3 reduce-scatter.7
